TPU v7x, 32 devices: a whole 2x2x4 slice. The times are simulated.
32 devices in a mesh: batch: 4 (over y, x), ctx: 4 (over z), wt: 2 (over core).
Axes of the slice: x: 2, y: 2, z: 4, core: 2. Of those that a mesh axis runs over, the one named last changes fastest.
Arguments:
- inputs: bfloat16 [8, 512, 768], P(('batch', 'wt'), 'ctx'), may hold values from -6 to 6
- prefix_keys: bfloat16 [8, 20, 768], P(('batch', 'wt')), may hold values from -8 to 8
- prefix_values: bfloat16 [8, 20, 768], P(('batch', 'wt')), may hold values from -6 to 6
- gain_attn: bfloat16 [768], P('wt'), may hold values from 0.099609375 to 1.8984375
- w_query: bfloat16 [768, 768], P('wt'), may hold values from -0.02734375 to 0.02734375
- w_key: bfloat16 [768, 768], P('wt'), may hold values from -0.21875 to 0.21875
- w_value: bfloat16 [768, 768], P('wt'), may hold values from -0.21875 to 0.21875
- w_out: bfloat16 [768, 768], P('wt'), may hold values from -2.5 to 2.5
- bias_table: bfloat16 [32, 12], P('wt'), may hold values from -5 to 5
- gain_ffn: bfloat16 [768], P('wt'), may hold values from 0.099609375 to 1.8984375
- w_in: bfloat16 [768, 3072], P('wt'), may hold values from -0.21875 to 0.21875
- w_back: bfloat16 [3072, 768], P('wt'), may hold values from -0.15625 to 0.15625
- buckets: int32 [1023], replicated, may hold values from 0 to 31
- out_grad: bfloat16 [8, 512, 768], P(('batch', 'wt'), 'ctx'), may hold values from -6 to 6
Outputs:
- outputs: bfloat16 [8, 512, 768], P(('batch', 'wt'), 'ctx')
- grad_inputs: bfloat16 [8, 512, 768], P(('batch', 'wt'), 'ctx')
- grad_prefix_keys: float32 [8, 20, 768], P(('batch', 'wt'))
- grad_prefix_values: float32 [8, 20, 768], P(('batch', 'wt'))
- grad_gain_attn: float32 [768], P('wt')
- grad_gain_ffn: float32 [768], P('wt')
- grad_bias_table: float32 [32, 12], P('wt')
- grad_query: float32 [768, 768], P('wt')
- grad_key: float32 [768, 768], P('wt')
- grad_value: float32 [768, 768], P('wt')
- grad_out: float32 [768, 768], P('wt')
- grad_in: float32 [768, 3072], P('wt')
- grad_back: float32 [3072, 768], P('wt')
All inputs are finite; a program needn't handle non-finite values.
Results may differ from a plain program's by a relative error of at most 0.028.
Values may be sent and summed in bfloat16 or wider, within the bound.
No kernel may reach another device: no remote copies, remote signals or barrier semaphores. Data moves between devices by JAX's collectives and lax.ppermute only.
A program may use at most 128 MiB of HBM per device.

v0:
```python
import jax
import jax.numpy as jnp
from jax import lax
from jax.sharding import PartitionSpec as P

KB = 256
EPS = 1e-06


def times_t(left, right):
    return lax.dot_general(
        left, right, (((1,), (1,)), ((), ())), preferred_element_type=jnp.float32
    )


def t_times(left, right):
    return lax.dot_general(
        left, right, (((0,), (0,)), ((), ())), preferred_element_type=jnp.float32
    )


def norm_parts(values):
    inverse = lax.rsqrt(jnp.mean(values * values, axis=-1, keepdims=True) + EPS)
    return (values * inverse, inverse)


def norm_back(grad_norm, gain, scaled, inverse):
    grad_scaled = grad_norm * gain
    return inverse * (grad_scaled - scaled * jnp.mean(grad_scaled * scaled, axis=-1, keepdims=True))


def smooth_act(values):
    return jax.nn.gelu(values, approximate=True)


def shards(
    inputs,
    prefix_keys,
    prefix_values,
    gain_attn,
    w_query,
    w_key,
    w_value,
    w_out,
    bias_table,
    gain_ffn,
    w_in,
    w_back,
    buckets,
    out_grad,
):
    wq, wk, wv, wo, gain_one, table = (
        lax.all_gather(w_query, "wt", axis=0, tiled=True),
        lax.all_gather(w_key, "wt", axis=0, tiled=True),
        lax.all_gather(w_value, "wt", axis=0, tiled=True),
        lax.all_gather(w_out, "wt", axis=0, tiled=True),
        lax.all_gather(gain_attn, "wt", axis=0, tiled=True),
        lax.all_gather(bias_table, "wt", axis=0, tiled=True),
    )
    w_first, w_second, gain_two = (
        lax.all_gather(w_in, "wt", axis=0, tiled=True),
        lax.all_gather(w_back, "wt", axis=0, tiled=True),
        lax.all_gather(gain_ffn, "wt", axis=0, tiled=True),
    )
    tokens = inputs[0].astype(jnp.float32)
    rows, width = tokens.shape
    heads = table.shape[1]
    nbuck = table.shape[0]
    hsize = width // heads
    memory = prefix_keys.shape[1]
    keys_mem = prefix_keys[0].reshape(memory, heads, hsize)
    vals_mem = prefix_values[0].reshape(memory, heads, hsize)
    scaled1, inverse1 = norm_parts(tokens)
    normed1 = (scaled1 * gain_one.astype(jnp.float32)).astype(jnp.bfloat16)
    query = jnp.dot(normed1, wq, preferred_element_type=jnp.float32).astype(jnp.bfloat16)
    keys = jnp.dot(normed1, wk, preferred_element_type=jnp.float32).astype(jnp.bfloat16)
    vals = jnp.dot(normed1, wv, preferred_element_type=jnp.float32).astype(jnp.bfloat16)
    key_full, value_full = (
        lax.all_gather(keys, "ctx", axis=0, tiled=True),
        lax.all_gather(vals, "ctx", axis=0, tiled=True),
    )
    length = key_full.shape[0]
    starts = jnp.arange(length // KB, dtype=jnp.int32) * KB
    bucket_range = jnp.arange(nbuck, dtype=jnp.int32)
    positions = lax.axis_index("ctx") * rows + jnp.arange(rows, dtype=jnp.int32)
    qheads = query.reshape(rows, heads, hsize)

    def scores_at(start, key_all):
        key_block = lax.dynamic_slice_in_dim(key_all, start, KB, 0).reshape(KB, heads, hsize)
        cols = start + jnp.arange(KB, dtype=jnp.int32)
        where = cols[None, :] - positions[:, None] + (length - 1)
        bucket_ids = buckets[where]
        bucket_map = (bucket_ids[:, :, None] == bucket_range[None, None, :]).astype(jnp.bfloat16)
        bias = jnp.einsum("qkb,bh->hqk", bucket_map, table, preferred_element_type=jnp.float32)
        raw = jnp.einsum("qhd,khd->hqk", qheads, key_block, preferred_element_type=jnp.float32)
        return (raw + bias, bucket_map, key_block)

    mem_scores = jnp.einsum("qhd,khd->hqk", qheads, keys_mem, preferred_element_type=jnp.float32)
    top_start = jnp.max(mem_scores, axis=2)
    total_start = jnp.sum(jnp.exp(mem_scores - top_start[:, :, None]), axis=2)

    def stat_step(carry, start):
        top, total = carry
        block, _, _ = scores_at(start, key_full)
        new_top = jnp.maximum(top, jnp.max(block, axis=2))
        total = total * jnp.exp(top - new_top) + jnp.sum(
            jnp.exp(block - new_top[:, :, None]), axis=2
        )
        return ((new_top, total), None)

    (top, total), _ = lax.scan(stat_step, (top_start, total_start), starts)
    mem_prob = jnp.exp(mem_scores - top[:, :, None]) / total[:, :, None]
    mem_low = mem_prob.astype(jnp.bfloat16)
    mixed_start = jnp.einsum("hqk,khd->qhd", mem_low, vals_mem, preferred_element_type=jnp.float32)

    def out_step(acc, start):
        block, _, _ = scores_at(start, key_full)
        prob = (jnp.exp(block - top[:, :, None]) / total[:, :, None]).astype(jnp.bfloat16)
        value_block = lax.dynamic_slice_in_dim(value_full, start, KB, 0).reshape(KB, heads, hsize)
        return (
            acc + jnp.einsum("hqk,khd->qhd", prob, value_block, preferred_element_type=jnp.float32),
            None,
        )

    mixed, _ = lax.scan(out_step, mixed_start, starts)
    attended = mixed.reshape(rows, width).astype(jnp.bfloat16)
    hidden = tokens + jnp.dot(attended, wo, preferred_element_type=jnp.float32)
    scaled2, inverse2 = norm_parts(hidden)
    normed2 = (scaled2 * gain_two.astype(jnp.float32)).astype(jnp.bfloat16)
    inner = jnp.dot(normed2, w_first, preferred_element_type=jnp.float32)
    act_value, act_pull = jax.vjp(smooth_act, inner)
    act_out = act_value.astype(jnp.bfloat16)
    result = hidden + jnp.dot(act_out, w_second, preferred_element_type=jnp.float32)
    wq, wk, wv, wo, gain_one = (
        lax.all_gather(w_query, "wt", axis=0, tiled=True),
        lax.all_gather(w_key, "wt", axis=0, tiled=True),
        lax.all_gather(w_value, "wt", axis=0, tiled=True),
        lax.all_gather(w_out, "wt", axis=0, tiled=True),
        lax.all_gather(gain_attn, "wt", axis=0, tiled=True),
    )
    w_first, w_second, gain_two = (
        lax.all_gather(w_in, "wt", axis=0, tiled=True),
        lax.all_gather(w_back, "wt", axis=0, tiled=True),
        lax.all_gather(gain_ffn, "wt", axis=0, tiled=True),
    )
    key_back, value_back = (
        lax.all_gather(keys, "ctx", axis=0, tiled=True),
        lax.all_gather(vals, "ctx", axis=0, tiled=True),
    )
    cotangent = out_grad[0]
    grad_second = t_times(act_out, cotangent)
    grad_act = times_t(cotangent, w_second).astype(jnp.bfloat16)
    grad_inner = act_pull(grad_act.astype(jnp.float32))[0].astype(jnp.bfloat16)
    grad_first = t_times(normed2, grad_inner)
    grad_normed2 = times_t(grad_inner, w_first)
    grad_gain_two = jnp.sum(grad_normed2 * scaled2, axis=0)
    grad_hidden = cotangent.astype(jnp.float32) + norm_back(
        grad_normed2, gain_two.astype(jnp.float32), scaled2, inverse2
    )
    part_first, part_second, part_gain_two = (
        lax.psum_scatter(
            grad_first.astype(jnp.bfloat16), "wt", scatter_dimension=0, tiled=True
        ).astype(jnp.float32),
        lax.psum_scatter(
            grad_second.astype(jnp.bfloat16), "wt", scatter_dimension=0, tiled=True
        ).astype(jnp.float32),
        lax.psum_scatter(
            grad_gain_two.astype(jnp.bfloat16), "wt", scatter_dimension=0, tiled=True
        ).astype(jnp.float32),
    )
    grad_branch = grad_hidden.astype(jnp.bfloat16)
    grad_wo = t_times(attended, grad_branch)
    grad_mixed = times_t(grad_branch, wo).astype(jnp.bfloat16).reshape(rows, heads, hsize)
    spread = jnp.einsum("qhd,qhd->hq", grad_mixed.astype(jnp.float32), mixed)
    mem_dprob = jnp.einsum("qhd,khd->hqk", grad_mixed, vals_mem, preferred_element_type=jnp.float32)
    mem_dscore = (mem_prob * (mem_dprob - spread[:, :, None])).astype(jnp.bfloat16)
    grad_q_start = jnp.einsum(
        "hqk,khd->qhd", mem_dscore, keys_mem, preferred_element_type=jnp.float32
    )
    grad_mem_keys = jnp.einsum(
        "hqk,qhd->khd", mem_dscore, qheads, preferred_element_type=jnp.float32
    ).reshape(memory, width)
    grad_mem_values = jnp.einsum(
        "hqk,qhd->khd", mem_low, grad_mixed, preferred_element_type=jnp.float32
    ).reshape(memory, width)

    def grad_step(carry, start):
        grad_q, table_acc = carry
        block, bucket_map, key_block = scores_at(start, key_back)
        prob = jnp.exp(block - top[:, :, None]) / total[:, :, None]
        value_block = lax.dynamic_slice_in_dim(value_back, start, KB, 0).reshape(KB, heads, hsize)
        grad_prob = jnp.einsum(
            "qhd,khd->hqk", grad_mixed, value_block, preferred_element_type=jnp.float32
        )
        grad_score = (prob * (grad_prob - spread[:, :, None])).astype(jnp.bfloat16)
        grad_q = grad_q + jnp.einsum(
            "hqk,khd->qhd", grad_score, key_block, preferred_element_type=jnp.float32
        )
        grad_kblock = jnp.einsum(
            "hqk,qhd->khd", grad_score, qheads, preferred_element_type=jnp.float32
        ).reshape(KB, width)
        grad_vblock = jnp.einsum(
            "hqk,qhd->khd",
            prob.astype(jnp.bfloat16),
            grad_mixed,
            preferred_element_type=jnp.float32,
        ).reshape(KB, width)
        table_acc = table_acc + jnp.einsum(
            "hqk,qkb->bh", grad_score, bucket_map, preferred_element_type=jnp.float32
        )
        return ((grad_q, table_acc), (grad_kblock, grad_vblock))

    zero_table = jnp.zeros((nbuck, heads), jnp.float32)
    (grad_q, grad_table), (grad_kblocks, grad_vblocks) = lax.scan(
        grad_step, (grad_q_start, zero_table), starts
    )
    grad_key_all = grad_kblocks.reshape(length, width)
    grad_value_all = grad_vblocks.reshape(length, width)
    grad_key_own, grad_value_own = (
        lax.psum_scatter(
            grad_key_all.astype(jnp.bfloat16), "ctx", scatter_dimension=0, tiled=True
        ).astype(jnp.float32),
        lax.psum_scatter(
            grad_value_all.astype(jnp.bfloat16), "ctx", scatter_dimension=0, tiled=True
        ).astype(jnp.float32),
    )
    mem_key_total, mem_value_total = (
        lax.psum(grad_mem_keys.astype(jnp.bfloat16), "ctx").astype(jnp.float32),
        lax.psum(grad_mem_values.astype(jnp.bfloat16), "ctx").astype(jnp.float32),
    )
    grad_q_low = grad_q.reshape(rows, width).astype(jnp.bfloat16)
    grad_k_low = grad_key_own.astype(jnp.bfloat16)
    grad_v_low = grad_value_own.astype(jnp.bfloat16)
    grad_wq = t_times(normed1, grad_q_low)
    grad_wk = t_times(normed1, grad_k_low)
    grad_wv = t_times(normed1, grad_v_low)
    grad_normed1 = times_t(grad_q_low, wq) + times_t(grad_k_low, wk) + times_t(grad_v_low, wv)
    grad_gain_one = jnp.sum(grad_normed1 * scaled1, axis=0)
    grad_tokens = grad_hidden + norm_back(
        grad_normed1, gain_one.astype(jnp.float32), scaled1, inverse1
    )
    part_wq, part_wk, part_wv, part_wo, part_gain_one, part_table = (
        lax.psum_scatter(
            grad_wq.astype(jnp.bfloat16), "wt", scatter_dimension=0, tiled=True
        ).astype(jnp.float32),
        lax.psum_scatter(
            grad_wk.astype(jnp.bfloat16), "wt", scatter_dimension=0, tiled=True
        ).astype(jnp.float32),
        lax.psum_scatter(
            grad_wv.astype(jnp.bfloat16), "wt", scatter_dimension=0, tiled=True
        ).astype(jnp.float32),
        lax.psum_scatter(
            grad_wo.astype(jnp.bfloat16), "wt", scatter_dimension=0, tiled=True
        ).astype(jnp.float32),
        lax.psum_scatter(
            grad_gain_one.astype(jnp.bfloat16), "wt", scatter_dimension=0, tiled=True
        ).astype(jnp.float32),
        lax.psum_scatter(
            grad_table.astype(jnp.bfloat16), "wt", scatter_dimension=0, tiled=True
        ).astype(jnp.float32),
    )
    sums = (
        lax.psum(part_wq.astype(jnp.bfloat16), ("batch", "ctx")).astype(jnp.float32),
        lax.psum(part_wk.astype(jnp.bfloat16), ("batch", "ctx")).astype(jnp.float32),
        lax.psum(part_wv.astype(jnp.bfloat16), ("batch", "ctx")).astype(jnp.float32),
        lax.psum(part_wo.astype(jnp.bfloat16), ("batch", "ctx")).astype(jnp.float32),
        lax.psum(part_gain_one.astype(jnp.bfloat16), ("batch", "ctx")).astype(jnp.float32),
        lax.psum(part_table.astype(jnp.bfloat16), ("batch", "ctx")).astype(jnp.float32),
        lax.psum(part_first.astype(jnp.bfloat16), ("batch", "ctx")).astype(jnp.float32),
        lax.psum(part_second.astype(jnp.bfloat16), ("batch", "ctx")).astype(jnp.float32),
        lax.psum(part_gain_two.astype(jnp.bfloat16), ("batch", "ctx")).astype(jnp.float32),
    )
    return (
        result.astype(jnp.bfloat16)[None],
        grad_tokens.astype(jnp.bfloat16)[None],
        mem_key_total[None],
        mem_value_total[None],
        sums[4],
        sums[8],
        sums[5],
        sums[0],
        sums[1],
        sums[2],
        sums[3],
        sums[6],
        sums[7],
    )


def solution(mesh):
    in_specs = (
        P(("batch", "wt"), "ctx", None),
        P(("batch", "wt"), None, None),
        P(("batch", "wt"), None, None),
        P("wt"),
        P("wt", None),
        P("wt", None),
        P("wt", None),
        P("wt", None),
        P("wt", None),
        P("wt"),
        P("wt", None),
        P("wt", None),
        P(),
        P(("batch", "wt"), "ctx", None),
    )
    out_specs = (
        P(("batch", "wt"), "ctx", None),
        P(("batch", "wt"), "ctx", None),
        P(("batch", "wt"), None, None),
        P(("batch", "wt"), None, None),
        P("wt"),
        P("wt"),
        P("wt", None),
        P("wt", None),
        P("wt", None),
        P("wt", None),
        P("wt", None),
        P("wt", None),
        P("wt", None),
    )
    return jax.shard_map(shards, mesh=mesh, in_specs=in_specs, out_specs=out_specs, check_vma=False)
```

profile of v0, /device:TPU:0, one launch (start us, length us, event | category | flops | bytes accessed | tf_op | source)
XLA Modules:
  0.0 1362.5 jit_solution(13265489076617069256)
XLA Ops:
  24.0 9.5 all-gather.11.cloned.1.call-done
  35.2 19.8 %all_gather.46 = bf16[512,768]{1,0:T(8,128)(2,1)S(1)} all-gather(bf16[128,768]{1,0:T(8,128)(2,1)S(1)} %convolution_convert_fusion.9), channel_id=1, replica_groups=mesh['batch'=4,'ctx'=4,'wt'=2] {'ctx'}, dimensions={0}, use_global_device_ids=true | all-gather | bytes 983040 | tf_op jit(solution)/shard_map/all_gather | solution.py:79
  58.3 283.1 %while.47 = (s32[]{:T(128)}, f32[12,128]{1,0:T(8,128)}, f32[12,128]{1,0:T(8,128)}, s32[2]{0:T(128)S(1)}, bf16[512,768]{0,1:T(8,128)(2,1)S(1)}, /*index=5*/bf16[1...) while((s32[]{:T(128)}, f32[12,128]{1,0:T(8,128)}, ...), condition=%wide.region_6.7_spmd.clone, body=%wide.region_3.6_spmd.clone.sunk | while | flops 78318976 | bytes 12339127 | solution.py:111
  59.8 130.0 %gather_fusion = s32[32768]{0:T(1024)S(1)} fusion(s32[1023]{0:T(1024)S(1)} %get-tuple-element.1205, s32[32768]{0:T(1024)S(1)} %broadcast_clamp_fusion.6), kind=kCustom, calls=%fused_computation.clone.clone.1 | custom fusion | bytes 393216 | tf_op jit(solution)/shard_map/while/body/eval_jaxpr/gather | solution.py:92
  201.3 130.0 %gather_fusion = s32[32768]{0:T(1024)S(1)} fusion(s32[1023]{0:T(1024)S(1)} %get-tuple-element.1205, s32[32768]{0:T(1024)S(1)} %broadcast_clamp_fusion.6), kind=kCustom, calls=%fused_computation.clone.clone.1 | custom fusion | bytes 393216 | tf_op jit(solution)/shard_map/while/body/eval_jaxpr/gather | solution.py:92
  343.1 18.4 %all_gather.49 = bf16[512,768]{1,0:T(8,128)(2,1)S(1)} all-gather(bf16[128,768]{1,0:T(8,128)(2,1)S(1)} %convolution_convert_fusion.8), channel_id=1, replica_groups=mesh['batch'=4,'ctx'=4,'wt'=2] {'ctx'}, dimensions={0}, use_global_device_ids=true | all-gather | bytes 983040 | tf_op jit(solution)/shard_map/all_gather | solution.py:80
  364.4 284.0 %while.48 = (s32[]{:T(128)}, f32[128,12,64]{0,2,1:T(8,128)}, s32[2]{0:T(128)S(1)}, bf16[512,768]{0,1:T(8,128)(2,1)}, bf16[512,768]{0,1:T(8,128)(2,1)S(1)}, /*ind...) while((s32[]{:T(128)}, f32[128,12,64]{0,2,1:T(8,128)}, ...), condition=%wide.region_8.9_spmd.clone, body=%wide.region_7.8_spmd.clone.sunk | while | flops 128745856 | bytes 12664803 | solution.py:125
  370.1 130.0 %gather_fusion.1 = s32[32768]{0:T(1024)S(1)} fusion(s32[1023]{0:T(1024)S(1)} %get-tuple-element.1245, s32[32768]{0:T(1024)S(1)} %broadcast_clamp_fusion.7), kind=kCustom, calls=%fused_computation.1.clone.clone.1 | custom fusion | bytes 393216 | tf_op jit(solution)/shard_map/while/body/eval_jaxpr/gather | solution.py:92
  512.1 130.0 %gather_fusion.1 = s32[32768]{0:T(1024)S(1)} fusion(s32[1023]{0:T(1024)S(1)} %get-tuple-element.1245, s32[32768]{0:T(1024)S(1)} %broadcast_clamp_fusion.7), kind=kCustom, calls=%fused_computation.1.clone.clone.1 | custom fusion | bytes 393216 | tf_op jit(solution)/shard_map/while/body/eval_jaxpr/gather | solution.py:92
  654.7 4.8 fusion.52
  668.4 294.8 %while.49 = (s32[]{:T(128)}, f32[128,12,64]{0,2,1:T(8,128)}, f32[32,12]{0,1:T(8,128)S(1)}, bf16[2,256,768]{2,1,0:T(8,128)(2,1)}, bf16[2,256,768]{2,1,0:T(8,128)(...) while((s32[]{:T(128)}, f32[128,12,64]{0,2,1:T(8,128)}, ...), condition=%wide.region_12.13_spmd.clone, body=%wide.region_11.12_spmd.clone.sunk | while | flops 307135616 | bytes 21652508 | solution.py:214
  672.0 130.0 %gather_fusion.2 = s32[32768]{0:T(1024)S(1)} fusion(s32[1023]{0:T(1024)S(1)} %get-tuple-element.1299, s32[32768]{0:T(1024)S(1)} %broadcast_clamp_fusion.8), kind=kCustom, calls=%fused_computation.2.clone.clone.1 | custom fusion | bytes 393216 | tf_op jit(solution)/shard_map/while/body/eval_jaxpr/gather | solution.py:92
  819.4 130.0 %gather_fusion.2 = s32[32768]{0:T(1024)S(1)} fusion(s32[1023]{0:T(1024)S(1)} %get-tuple-element.1299, s32[32768]{0:T(1024)S(1)} %broadcast_clamp_fusion.8), kind=kCustom, calls=%fused_computation.2.clone.clone.1 | custom fusion | bytes 393216 | tf_op jit(solution)/shard_map/while/body/eval_jaxpr/gather | solution.py:92
  968.4 17.5 %reduce-scatter.12.cloned.1.call-done = bf16[128,768]{1,0:T(8,128)(2,1)} async-done(((bf16[512,768]{1,0:T(8,128)(2,1)}), bf16[128,768]{1,0:T(8,128)(2,1)}) %reduce-scatter.12.cloned.1.call-update) | async-done | bytes 196624 | tf_op jit(solution)/shard_map/reduce_scatter | solution.py:220
  988.6 22.8 %reduce-scatter.14.cloned.1.call-done = bf16[128,768]{1,0:T(8,128)(2,1)} async-done(((bf16[512,768]{1,0:T(8,128)(2,1)}), bf16[128,768]{1,0:T(8,128)(2,1)}) %reduce-scatter.14.cloned.1.call-update) | async-done | bytes 196624 | tf_op jit(solution)/shard_map/reduce_scatter | solution.py:223
  1023.8 11.0 reduce-scatter.22.cloned.1.call-done
  1034.8 12.7 reduce-scatter.18.cloned.1.call-done
  1047.6 12.6 reduce-scatter.20.cloned.1.call-done
  1060.2 16.7 %reduce-scatter.24.cloned.1.call-done = bf16[384,3072]{1,0:T(8,128)(2,1)} async-done(((bf16[768,3072]{1,0:T(8,128)(2,1)}), bf16[384,3072]{1,0:T(8,128)(2,1)}) %reduce-scatter.24.cloned.1.call-update) | async-done | bytes 2359312 | tf_op jit(solution)/shard_map/reduce_scatter | solution.py:161
  1076.9 16.6 %reduce-scatter.26.cloned.1.call-done = bf16[1536,768]{1,0:T(8,128)(2,1)} async-done(((bf16[3072,768]{1,0:T(8,128)(2,1)}), bf16[1536,768]{1,0:T(8,128)(2,1)}) %reduce-scatter.26.cloned.1.call-update) | async-done | bytes 2359312 | tf_op jit(solution)/shard_map/reduce_scatter | solution.py:164
  1098.1 20.5 %all-reduce.4 = (bf16[1,20,768]{2,1,0:T(8,128)(2,1)S(1)}, bf16[1,20,768]{2,1,0:T(8,128)(2,1)S(1)}) all-reduce(bf16[1,20,768]{2,1,0:T(8,128)(2,1)S(1)} %broadcast_in_dim.44, bf16[1,20,768]{2,1,0:T(8,128)(2,1)S(1)} %broadcast_in_dim.55), channel_id=1, replica_groups=mesh['batch'=4,'ctx'=4,'wt'=2] {'ctx'}, use_global_device_ids=true, to_apply=%region_16.17 | all-reduce | flops 30720 | bytes 122880 | tf_op jit(solution)/shard_map/psum | solution.py:228
  1121.8 4.1 fusion.54
  1131.9 42.3 %all-reduce.2 = (bf16[16,12]{0,1:T(8,128)(2,1)S(1)}, bf16[384]{0:T(512)(128)(2,1)S(1)}, bf16[384]{0:T(512)(128)(2,1)S(1)}) all-reduce(bf16[16,12]{0,1:T(8,128)(2,1)S(1)} %copy.182, bf16[384]{0:T(512)(128)(2,1)S(1)} %dynamic-slice.1, bf16[384]{0:T(512)(128)(2,1)S(1)} %dynamic-slice.3), channel_id=1, replica_groups=mesh['batch'=4,'ctx'=4,'wt'=2] {'batch','ctx'}, use_global_device_ids=true, to_apply=%region_25.26 | all-reduce | flops 960 | bytes 3840 | tf_op jit(solution)/shard_map/psum | solution.py:268
  1176.9 168.2 %all-reduce.8.cloned.1.call-done = (bf16[384,768]{1,0:T(8,128)(2,1)}, bf16[384,768]{1,0:T(8,128)(2,1)}, bf16[384,768]{1,0:T(8,128)(2,1)}, bf16[384,768]{1,0:T(8,...) async-done(((bf16[384,768]{1,0:T(8,128)(2,1)}, bf16[384,768]{1,0:T(8,128)(2,1)}, bf16[384,768]{1,0:T(8,128)(2,1)}, bf16[384,768]{1,0:T(8,128)(2,1)}, ...) | async-done | bytes 7077904 | tf_op jit(solution)/shard_map/psum | solution.py:263
  (326 shorter events, 157.0 us)
Async XLA Ops:
  7.2 14.3 %all-gather.9.cloned.1.call-start = ((), (), s32[]{:S(2)}) async-start(), calls=%async_computation.9 | async-start | bytes 1769472 | tf_op jit(solution)/shard_map/all_gather | solution.py:53
  7.9 25.6 %all-gather.11.cloned.1.call-start = ((), (), s32[]{:S(2)}) async-start(), calls=%async_computation.10 | async-start | bytes 1769472 | tf_op jit(solution)/shard_map/all_gather | solution.py:54
  8.7 332.8 %all-gather.13.cloned.1.call-start = ((), (), s32[]{:S(2)}) async-start(), calls=%async_computation.11 | async-start | bytes 1769472 | tf_op jit(solution)/shard_map/all_gather | solution.py:55
  9.4 640.1 %all-gather.15.cloned.1.call-start = ((), (), s32[]{:S(2)}) async-start(), calls=%async_computation.12 | async-start | bytes 1769472 | tf_op jit(solution)/shard_map/all_gather | solution.py:56
  10.0 641.4 %all-gather.17.cloned.1.call-start = ((), (), s32[]{:S(2)}) async-start(), calls=%async_computation.13 | async-start | bytes 7077888 | tf_op jit(solution)/shard_map/all_gather | solution.py:61
  10.6 644.0 %all-gather.19.cloned.1.call-start = ((), (), s32[]{:S(2)}) async-start(), calls=%async_computation.14 | async-start | bytes 7077888 | tf_op jit(solution)/shard_map/all_gather | solution.py:62
  11.2 974.7 %reduce-scatter.12.cloned.1.call-start = ((), (), s32[]{:S(2)}) async-start(), calls=%async_computation.15 | async-start | bytes 983040 | tf_op jit(solution)/shard_map/reduce_scatter | solution.py:220
  14.3 40.9 %copy-start.27 = (bf16[20,12,64]{2,1,0:T(8,128)(2,1)}, bf16[20,12,64]{2,1,0:T(8,128)(2,1)S(1)}, u32[]{:S(2)}) copy-start(bf16[20,12,64]{2,1,0:T(8,128)(2,1)S(1)} %reshape_squeeze.6) | copy-start | bytes 92164
  58.3 283.1 %copy-start.2 = (bf16[1,128,768]{2,1,0:T(8,128)(2,1)S(1)}, bf16[1,128,768]{2,1,0:T(8,128)(2,1)}, u32[]{:S(2)}) copy-start(bf16[1,128,768]{2,1,0:T(8,128)(2,1)} %param.20) | copy-start | bytes 589828
  58.3 283.1 %copy-start.37 = (f32[768]{0:T(1024)S(1)}, f32[768]{0:T(1024)}, u32[]{:S(2)}) copy-start(f32[768]{0:T(1024)} %copy-done.36) | copy-start | bytes 9220
  58.3 283.1 %copy-start.48 = (f32[128]{0:T(128)S(1)}, f32[128]{0:T(128)}, u32[]{:S(2)}) copy-start(f32[128]{0:T(128)} %copy-done.47) | copy-start | bytes 1540
  364.4 285.1 %copy-start.3 = (bf16[1,128,768]{2,1,0:T(8,128)(2,1)S(1)}, bf16[1,128,768]{2,1,0:T(8,128)(2,1)}, u32[]{:S(2)}) copy-start(bf16[1,128,768]{2,1,0:T(8,128)(2,1)} %param.20) | copy-start | bytes 589828
  963.3 48.2 %reduce-scatter.14.cloned.1.call-start = ((), (), s32[]{:S(2)}) async-start(), calls=%async_computation.16 | async-start | bytes 983040 | tf_op jit(solution)/shard_map/reduce_scatter | solution.py:223
  964.0 59.8 %reduce-scatter.16.cloned.1.call-start = ((), (), s32[]{:S(2)}) async-start(), calls=%async_computation.17 | async-start | bytes 1769472 | tf_op jit(solution)/shard_map/reduce_scatter | solution.py:243
  966.8 68.0 %reduce-scatter.22.cloned.1.call-start = ((), (), s32[]{:S(2)}) async-start(), calls=%async_computation.20 | async-start | bytes 1769472 | tf_op jit(solution)/shard_map/reduce_scatter | solution.py:252
  968.4 79.2 %reduce-scatter.18.cloned.1.call-start = ((), (), s32[]{:S(2)}) async-start(), calls=%async_computation.18 | async-start | bytes 1769472 | tf_op jit(solution)/shard_map/reduce_scatter | solution.py:246
  988.5 25.5 %copy-start.8 = (f32[128,768]{1,0:T(8,128)S(1)}, f32[128,768]{1,0:T(8,128)}, u32[]{:S(2)}) copy-start(f32[128,768]{1,0:T(8,128)} %copy-done.7) | copy-start | bytes 1179652
  988.5 25.5 %copy-start.17 = (bf16[128,3072]{1,0:T(8,128)(2,1)S(1)}, bf16[128,3072]{1,0:T(8,128)(2,1)}, u32[]{:S(2)}) copy-start(bf16[128,3072]{1,0:T(8,128)(2,1)} %copy-done.16) | copy-start | bytes 2359300
  988.5 25.5 %copy-start.42 = (f32[768]{0:T(1024)S(1)}, f32[768]{0:T(1024)}, u32[]{:S(2)}) copy-start(f32[768]{0:T(1024)} %reshape.356) | copy-start | bytes 9220
  988.5 71.7 %reduce-scatter.20.cloned.1.call-start = ((), (), s32[]{:S(2)}) async-start(), calls=%async_computation.19 | async-start | bytes 1769472 | tf_op jit(solution)/shard_map/reduce_scatter | solution.py:249
  1014.0 63.0 %reduce-scatter.24.cloned.1.call-start = ((), (), s32[]{:S(2)}) async-start(), calls=%async_computation.21 | async-start | bytes 7077888 | tf_op jit(solution)/shard_map/reduce_scatter | solution.py:161
  1017.7 75.8 %reduce-scatter.26.cloned.1.call-start = ((), (), s32[]{:S(2)}) async-start(), calls=%async_computation.22 | async-start | bytes 7077888 | tf_op jit(solution)/shard_map/reduce_scatter | solution.py:164
  1023.0 102.9 %reduce-scatter.28.cloned.1.call-start = ((), (), s32[]{:S(2)}) async-start(), calls=%async_computation.23 | async-start | bytes 12288
  1023.7 321.3 %all-reduce.8.cloned.1.call-start = ((), (), s32[]{:S(2)}) async-start(), calls=%async_computation.24 | async-start | bytes 14155776 | tf_op jit(solution)/shard_map/psum | solution.py:263
  (52 other events, 262.4 us)
Sparse Core Ops, SparseCore 0:
  9.6 11.9 all-gather.8
  23.1 10.3 all-gather.10
  35.0 10.3 all-gather.12
  46.9 10.3 all-gather.14
  58.7 15.5 all-gather.16
  75.7 15.6 all-gather.18
  963.4 22.5 reduce-scatter.11
  988.8 22.5 reduce-scatter.13
  1014.2 7.9 reduce-scatter.15
  1025.0 9.8 reduce-scatter.21
  1037.7 9.8 reduce-scatter.17
  1050.3 9.8 reduce-scatter.19
  1063.1 13.7 reduce-scatter.23
  1079.7 13.7 reduce-scatter.25
  1095.6 8.5 reduce-scatter.27
  1110.5 234.5 all-reduce.7
where the time goes:
time: 1360 us
  local copies, waits for them, and re-layouts  816 us (60%)
  waiting for transfers between devices  295 us (22%)
  blocking collectives  109 us (8%)
  matrix products  87.6 us (6%)
  other arithmetic  27.3 us (2%)
  between operations  15.4 us (1%)
    gather x14, local copies, waits for them, and re-layouts, scores_at(): bucket_ids = buckets[where]  781 us
    psum x1, waiting for transfers between devices, shards(): lax.psum(part_wq.astype(jnp.bfloat16), ('batch', 'ctx')).astype(jnp.float32)  168 us
    psum x1, blocking collectives, shards(): lax.psum(part_table.astype(jnp.bfloat16), ('batch', 'ctx'))  42.3 us
  transfers between devices with their start and end apart: 16, of which 10 were waited for; matrix products, arithmetic and copies ran while one was open for 45% of the time, Pallas kernels for 0%

commit v1 on v0

--- a/solution.py
+++ b/solution.py
@@ -265,7 +265,9 @@
         lax.psum(part_wv.astype(jnp.bfloat16), ("batch", "ctx")).astype(jnp.float32),
         lax.psum(part_wo.astype(jnp.bfloat16), ("batch", "ctx")).astype(jnp.float32),
         lax.psum(part_gain_one.astype(jnp.bfloat16), ("batch", "ctx")).astype(jnp.float32),
-        lax.psum(part_table.astype(jnp.bfloat16), ("batch", "ctx")).astype(jnp.float32),
+        jnp.sum(lax.all_gather(part_table.astype(jnp.bfloat16), ("batch", "ctx")), axis=0).astype(
+            jnp.float32
+        ),
         lax.psum(part_first.astype(jnp.bfloat16), ("batch", "ctx")).astype(jnp.float32),
         lax.psum(part_second.astype(jnp.bfloat16), ("batch", "ctx")).astype(jnp.float32),
         lax.psum(part_gain_two.astype(jnp.bfloat16), ("batch", "ctx")).astype(jnp.float32),

time: 1360 us -> 1360 us (level)
  blocking collectives: 109 us -> 145 us
  waiting for transfers between devices: 295 us -> 259 us
    all_gather x0 -> x1, blocking collectives: none -> 40.5 us  [shards(): lax.all_gather(part_table.astype(jnp.bfloat16), ('batch', 'ctx'))]
    psum x1, waiting for transfers between devices: 168 us -> 132 us  [shards(): lax.psum(part_wq.astype(jnp.bfloat16), ('batch', 'ctx')).astype(jnp.float32)]
where the time goes in v1:
time: 1360 us
  local copies, waits for them, and re-layouts  815 us (60%)
  waiting for transfers between devices  259 us (19%)
  blocking collectives  145 us (11%)
  matrix products  87.5 us (6%)
  other arithmetic  27.5 us (2%)
  between operations  15.3 us (1%)
    gather x14, local copies, waits for them, and re-layouts, scores_at(): bucket_ids = buckets[where]  781 us
    psum x1, waiting for transfers between devices, shards(): lax.psum(part_wq.astype(jnp.bfloat16), ('batch', 'ctx')).astype(jnp.float32)  132 us
    all_gather x1, blocking collectives, shards(): lax.all_gather(part_table.astype(jnp.bfloat16), ('batch', 'ctx'))  40.5 us
    psum x1, blocking collectives, shards(): lax.psum(part_gain_one.astype(jnp.bfloat16), ('batch', 'ctx'))  37.9 us
  transfers between devices with their start and end apart: 16, of which 10 were waited for; matrix products, arithmetic and copies ran while one was open for 45% of the time, Pallas kernels for 0%

profile of v1, /device:TPU:0, one launch (start us, length us, event | category | flops | bytes accessed | tf_op | source)
XLA Modules:
  0.0 1362.5 jit_solution(7263212093294375543)
XLA Ops:
  24.0 9.5 all-gather.12.cloned.1.call-done
  35.2 19.8 %all_gather.52 = bf16[512,768]{1,0:T(8,128)(2,1)S(1)} all-gather(bf16[128,768]{1,0:T(8,128)(2,1)S(1)} %convolution_convert_fusion.9), channel_id=1, replica_groups=mesh['batch'=4,'ctx'=4,'wt'=2] {'ctx'}, dimensions={0}, use_global_device_ids=true | all-gather | bytes 983040 | tf_op jit(solution)/shard_map/all_gather | solution.py:79
  58.3 283.1 %while.47 = (s32[]{:T(128)}, f32[12,128]{1,0:T(8,128)}, f32[12,128]{1,0:T(8,128)}, s32[2]{0:T(128)S(1)}, bf16[512,768]{0,1:T(8,128)(2,1)S(1)}, /*index=5*/bf16[1...) while((s32[]{:T(128)}, f32[12,128]{1,0:T(8,128)}, ...), condition=%wide.region_6.7_spmd.clone, body=%wide.region_3.6_spmd.clone.sunk | while | flops 78318976 | bytes 12339127 | solution.py:111
  59.8 130.0 %gather_fusion = s32[32768]{0:T(1024)S(1)} fusion(s32[1023]{0:T(1024)S(1)} %get-tuple-element.1106, s32[32768]{0:T(1024)S(1)} %broadcast_clamp_fusion.6), kind=kCustom, calls=%fused_computation.clone.clone.1 | custom fusion | bytes 393216 | tf_op jit(solution)/shard_map/while/body/eval_jaxpr/gather | solution.py:92
  201.3 130.0 %gather_fusion = s32[32768]{0:T(1024)S(1)} fusion(s32[1023]{0:T(1024)S(1)} %get-tuple-element.1106, s32[32768]{0:T(1024)S(1)} %broadcast_clamp_fusion.6), kind=kCustom, calls=%fused_computation.clone.clone.1 | custom fusion | bytes 393216 | tf_op jit(solution)/shard_map/while/body/eval_jaxpr/gather | solution.py:92
  343.1 18.4 %all_gather.55 = bf16[512,768]{1,0:T(8,128)(2,1)S(1)} all-gather(bf16[128,768]{1,0:T(8,128)(2,1)S(1)} %convolution_convert_fusion.8), channel_id=1, replica_groups=mesh['batch'=4,'ctx'=4,'wt'=2] {'ctx'}, dimensions={0}, use_global_device_ids=true | all-gather | bytes 983040 | tf_op jit(solution)/shard_map/all_gather | solution.py:80
  364.4 284.0 %while.48 = (s32[]{:T(128)}, f32[128,12,64]{0,2,1:T(8,128)}, s32[2]{0:T(128)S(1)}, bf16[512,768]{0,1:T(8,128)(2,1)}, bf16[512,768]{0,1:T(8,128)(2,1)S(1)}, /*ind...) while((s32[]{:T(128)}, f32[128,12,64]{0,2,1:T(8,128)}, ...), condition=%wide.region_8.9_spmd.clone, body=%wide.region_7.8_spmd.clone.sunk | while | flops 128745856 | bytes 12664803 | solution.py:125
  370.1 130.0 %gather_fusion.1 = s32[32768]{0:T(1024)S(1)} fusion(s32[1023]{0:T(1024)S(1)} %get-tuple-element.1146, s32[32768]{0:T(1024)S(1)} %broadcast_clamp_fusion.7), kind=kCustom, calls=%fused_computation.1.clone.clone.1 | custom fusion | bytes 393216 | tf_op jit(solution)/shard_map/while/body/eval_jaxpr/gather | solution.py:92
  512.1 130.0 %gather_fusion.1 = s32[32768]{0:T(1024)S(1)} fusion(s32[1023]{0:T(1024)S(1)} %get-tuple-element.1146, s32[32768]{0:T(1024)S(1)} %broadcast_clamp_fusion.7), kind=kCustom, calls=%fused_computation.1.clone.clone.1 | custom fusion | bytes 393216 | tf_op jit(solution)/shard_map/while/body/eval_jaxpr/gather | solution.py:92
  654.7 4.8 fusion.52
  668.4 295.4 %while.49 = (s32[]{:T(128)}, f32[128,12,64]{0,2,1:T(8,128)}, f32[32,12]{0,1:T(8,128)S(1)}, bf16[2,256,768]{2,1,0:T(8,128)(2,1)}, bf16[2,256,768]{2,1,0:T(8,128)(...) while((s32[]{:T(128)}, f32[128,12,64]{0,2,1:T(8,128)}, ...), condition=%wide.region_12.13_spmd.clone, body=%wide.region_11.12_spmd.clone.sunk | while | flops 307135616 | bytes 21652508 | solution.py:214
  672.2 130.0 %gather_fusion.2 = s32[32768]{0:T(1024)S(1)} fusion(s32[1023]{0:T(1024)S(1)} %get-tuple-element.1200, s32[32768]{0:T(1024)S(1)} %broadcast_clamp_fusion.8), kind=kCustom, calls=%fused_computation.2.clone.clone.1 | custom fusion | bytes 393216 | tf_op jit(solution)/shard_map/while/body/eval_jaxpr/gather | solution.py:92
  820.0 130.0 %gather_fusion.2 = s32[32768]{0:T(1024)S(1)} fusion(s32[1023]{0:T(1024)S(1)} %get-tuple-element.1200, s32[32768]{0:T(1024)S(1)} %broadcast_clamp_fusion.8), kind=kCustom, calls=%fused_computation.2.clone.clone.1 | custom fusion | bytes 393216 | tf_op jit(solution)/shard_map/while/body/eval_jaxpr/gather | solution.py:92
  969.0 17.6 %reduce-scatter.12.cloned.1.call-done = bf16[128,768]{1,0:T(8,128)(2,1)} async-done(((bf16[512,768]{1,0:T(8,128)(2,1)}), bf16[128,768]{1,0:T(8,128)(2,1)}) %reduce-scatter.12.cloned.1.call-update) | async-done | bytes 196624 | tf_op jit(solution)/shard_map/reduce_scatter | solution.py:220
  989.2 22.8 %reduce-scatter.14.cloned.1.call-done = bf16[128,768]{1,0:T(8,128)(2,1)} async-done(((bf16[512,768]{1,0:T(8,128)(2,1)}), bf16[128,768]{1,0:T(8,128)(2,1)}) %reduce-scatter.14.cloned.1.call-update) | async-done | bytes 196624 | tf_op jit(solution)/shard_map/reduce_scatter | solution.py:223
  1024.5 11.0 reduce-scatter.22.cloned.1.call-done
  1035.5 12.7 reduce-scatter.18.cloned.1.call-done
  1048.2 12.7 reduce-scatter.20.cloned.1.call-done
  1060.9 16.7 %reduce-scatter.24.cloned.1.call-done = bf16[384,3072]{1,0:T(8,128)(2,1)} async-done(((bf16[768,3072]{1,0:T(8,128)(2,1)}), bf16[384,3072]{1,0:T(8,128)(2,1)}) %reduce-scatter.24.cloned.1.call-update) | async-done | bytes 2359312 | tf_op jit(solution)/shard_map/reduce_scatter | solution.py:161
  1077.6 16.6 %reduce-scatter.26.cloned.1.call-done = bf16[1536,768]{1,0:T(8,128)(2,1)} async-done(((bf16[3072,768]{1,0:T(8,128)(2,1)}), bf16[1536,768]{1,0:T(8,128)(2,1)}) %reduce-scatter.26.cloned.1.call-update) | async-done | bytes 2359312 | tf_op jit(solution)/shard_map/reduce_scatter | solution.py:164
  1098.8 20.5 %all-reduce.4 = (bf16[1,20,768]{2,1,0:T(8,128)(2,1)S(1)}, bf16[1,20,768]{2,1,0:T(8,128)(2,1)S(1)}) all-reduce(bf16[1,20,768]{2,1,0:T(8,128)(2,1)S(1)} %broadcast_in_dim.44, bf16[1,20,768]{2,1,0:T(8,128)(2,1)S(1)} %broadcast_in_dim.55), channel_id=1, replica_groups=mesh['batch'=4,'ctx'=4,'wt'=2] {'ctx'}, use_global_device_ids=true, to_apply=%region_16.17 | all-reduce | flops 30720 | bytes 122880 | tf_op jit(solution)/shard_map/psum | solution.py:228
  1126.6 40.5 %all-gather = bf16[256,12]{1,0:T(8,128)(2,1)S(1)} all-gather(bf16[16,12]{1,0:T(8,128)(2,1)} %reduce-scatter.28.cloned.1.call-done), channel_id=2, replica_groups=mesh['batch'=4,'ctx'=4,'wt'=2] {'batch','ctx'}, dimensions={0}, use_global_device_ids=true | all-gather | bytes 6528 | tf_op jit(solution)/shard_map/all_gather | solution.py:268
  1173.0 37.9 %all-reduce.2 = (bf16[384]{0:T(512)(128)(2,1)S(1)}, bf16[384]{0:T(512)(128)(2,1)S(1)}) all-reduce(bf16[384]{0:T(512)(128)(2,1)S(1)} %dynamic-slice.1, bf16[384]{0:T(512)(128)(2,1)S(1)} %dynamic-slice.3), channel_id=1, replica_groups=mesh['batch'=4,'ctx'=4,'wt'=2] {'batch','ctx'}, use_global_device_ids=true, to_apply=%region_20.21 | all-reduce | flops 768 | bytes 3072 | tf_op jit(solution)/shard_map/psum | solution.py:267
  1213.0 132.1 %all-reduce.8.cloned.1.call-done = (bf16[384,768]{1,0:T(8,128)(2,1)}, bf16[384,768]{1,0:T(8,128)(2,1)}, bf16[384,768]{1,0:T(8,128)(2,1)}, bf16[384,768]{1,0:T(8,...) async-done(((bf16[384,768]{1,0:T(8,128)(2,1)}, bf16[384,768]{1,0:T(8,128)(2,1)}, bf16[384,768]{1,0:T(8,128)(2,1)}, bf16[384,768]{1,0:T(8,128)(2,1)}, ...) | async-done | bytes 7077904 | tf_op jit(solution)/shard_map/psum | solution.py:263
  (328 shorter events, 160.6 us)
Async XLA Ops:
  7.2 14.3 %all-gather.10.cloned.1.call-start = ((), (), s32[]{:S(2)}) async-start(), calls=%async_computation.9 | async-start | bytes 1769472 | tf_op jit(solution)/shard_map/all_gather | solution.py:53
  7.9 25.6 %all-gather.12.cloned.1.call-start = ((), (), s32[]{:S(2)}) async-start(), calls=%async_computation.10 | async-start | bytes 1769472 | tf_op jit(solution)/shard_map/all_gather | solution.py:54
  8.7 332.7 %all-gather.14.cloned.1.call-start = ((), (), s32[]{:S(2)}) async-start(), calls=%async_computation.11 | async-start | bytes 1769472 | tf_op jit(solution)/shard_map/all_gather | solution.py:55
  9.4 640.1 %all-gather.16.cloned.1.call-start = ((), (), s32[]{:S(2)}) async-start(), calls=%async_computation.12 | async-start | bytes 1769472 | tf_op jit(solution)/shard_map/all_gather | solution.py:56
  10.0 641.4 %all-gather.18.cloned.1.call-start = ((), (), s32[]{:S(2)}) async-start(), calls=%async_computation.13 | async-start | bytes 7077888 | tf_op jit(solution)/shard_map/all_gather | solution.py:61
  10.6 644.0 %all-gather.20.cloned.1.call-start = ((), (), s32[]{:S(2)}) async-start(), calls=%async_computation.14 | async-start | bytes 7077888 | tf_op jit(solution)/shard_map/all_gather | solution.py:62
  11.2 975.4 %reduce-scatter.12.cloned.1.call-start = ((), (), s32[]{:S(2)}) async-start(), calls=%async_computation.15 | async-start | bytes 983040 | tf_op jit(solution)/shard_map/reduce_scatter | solution.py:220
  14.3 40.9 %copy-start.27 = (bf16[20,12,64]{2,1,0:T(8,128)(2,1)}, bf16[20,12,64]{2,1,0:T(8,128)(2,1)S(1)}, u32[]{:S(2)}) copy-start(bf16[20,12,64]{2,1,0:T(8,128)(2,1)S(1)} %reshape_squeeze.6) | copy-start | bytes 92164
  58.3 283.1 %copy-start.2 = (bf16[1,128,768]{2,1,0:T(8,128)(2,1)S(1)}, bf16[1,128,768]{2,1,0:T(8,128)(2,1)}, u32[]{:S(2)}) copy-start(bf16[1,128,768]{2,1,0:T(8,128)(2,1)} %param.20) | copy-start | bytes 589828
  58.3 283.1 %copy-start.37 = (f32[768]{0:T(1024)S(1)}, f32[768]{0:T(1024)}, u32[]{:S(2)}) copy-start(f32[768]{0:T(1024)} %copy-done.36) | copy-start | bytes 9220
  58.3 283.1 %copy-start.48 = (f32[128]{0:T(128)S(1)}, f32[128]{0:T(128)}, u32[]{:S(2)}) copy-start(f32[128]{0:T(128)} %copy-done.47) | copy-start | bytes 1540
  364.4 285.1 %copy-start.3 = (bf16[1,128,768]{2,1,0:T(8,128)(2,1)S(1)}, bf16[1,128,768]{2,1,0:T(8,128)(2,1)}, u32[]{:S(2)}) copy-start(bf16[1,128,768]{2,1,0:T(8,128)(2,1)} %param.20) | copy-start | bytes 589828
  963.8 48.3 %reduce-scatter.14.cloned.1.call-start = ((), (), s32[]{:S(2)}) async-start(), calls=%async_computation.16 | async-start | bytes 983040 | tf_op jit(solution)/shard_map/reduce_scatter | solution.py:223
  964.6 59.9 %reduce-scatter.16.cloned.1.call-start = ((), (), s32[]{:S(2)}) async-start(), calls=%async_computation.17 | async-start | bytes 1769472 | tf_op jit(solution)/shard_map/reduce_scatter | solution.py:243
  967.4 68.2 %reduce-scatter.22.cloned.1.call-start = ((), (), s32[]{:S(2)}) async-start(), calls=%async_computation.20 | async-start | bytes 1769472 | tf_op jit(solution)/shard_map/reduce_scatter | solution.py:252
  968.9 79.3 %reduce-scatter.18.cloned.1.call-start = ((), (), s32[]{:S(2)}) async-start(), calls=%async_computation.18 | async-start | bytes 1769472 | tf_op jit(solution)/shard_map/reduce_scatter | solution.py:246
  989.2 71.7 %reduce-scatter.20.cloned.1.call-start = ((), (), s32[]{:S(2)}) async-start(), calls=%async_computation.19 | async-start | bytes 1769472 | tf_op jit(solution)/shard_map/reduce_scatter | solution.py:249
  1014.6 63.0 %reduce-scatter.24.cloned.1.call-start = ((), (), s32[]{:S(2)}) async-start(), calls=%async_computation.21 | async-start | bytes 7077888 | tf_op jit(solution)/shard_map/reduce_scatter | solution.py:161
  1018.4 75.8 %reduce-scatter.26.cloned.1.call-start = ((), (), s32[]{:S(2)}) async-start(), calls=%async_computation.22 | async-start | bytes 7077888 | tf_op jit(solution)/shard_map/reduce_scatter | solution.py:164
  1023.6 102.9 %reduce-scatter.28.cloned.1.call-start = ((), (), s32[]{:S(2)}) async-start(), calls=%async_computation.23 | async-start | bytes 12288 | tf_op jit(solution)/shard_map/reduce_scatter | solution.py:258
  1024.4 320.7 %all-reduce.8.cloned.1.call-start = ((), (), s32[]{:S(2)}) async-start(), calls=%async_computation.24 | async-start | bytes 14155776 | tf_op jit(solution)/shard_map/psum | solution.py:263
  1122.4 45.5 %copy-start.23 = (bf16[128,768]{1,0:T(8,128)(2,1)S(1)}, bf16[128,768]{1,0:T(8,128)(2,1)}, u32[]{:S(2)}) copy-start(bf16[128,768]{1,0:T(8,128)(2,1)} %reduce-scatter.12.cloned.1.call-done) | copy-start | bytes 589828
  1126.6 43.2 %copy-start.14 = (bf16[768,768]{1,0:T(8,128)(2,1)S(1)}, bf16[768,768]{1,0:T(8,128)(2,1)}, u32[]{:S(2)}) copy-start(bf16[768,768]{1,0:T(8,128)(2,1)} %all-gather.14.cloned.1.call-done) | copy-start | bytes 3538948
  1126.6 43.2 %copy-start.24 = (bf16[128,768]{1,0:T(8,128)(2,1)S(1)}, bf16[128,768]{1,0:T(8,128)(2,1)}, u32[]{:S(2)}) copy-start(bf16[128,768]{1,0:T(8,128)(2,1)} %reduce-scatter.14.cloned.1.call-done) | copy-start | bytes 589828
  (52 other events, 328.6 us)
Sparse Core Ops, SparseCore 0:
  9.6 11.9 all-gather.9
  23.1 10.3 all-gather.11
  35.0 10.3 all-gather.13
  46.9 10.3 all-gather.15
  58.7 15.5 all-gather.17
  75.7 15.6 all-gather.19
  963.9 22.6 reduce-scatter.11
  989.5 22.5 reduce-scatter.13
  1014.9 7.9 reduce-scatter.15
  1025.6 9.8 reduce-scatter.21
  1038.4 9.8 reduce-scatter.17
  1051.0 9.8 reduce-scatter.19
  1063.8 13.7 reduce-scatter.23
  1080.4 13.7 reduce-scatter.25
  1096.3 8.5 reduce-scatter.27
  1111.2 233.9 all-reduce.7
